TPU v7x, 32 devices: a whole 2x2x4 slice. The times are simulated.
32 devices in a mesh: groups: 2 (over x), seq: 16 (over z, y, core).
Axes of the slice: x: 2, y: 2, z: 4, core: 2. Of those that a mesh axis runs over, the one named last changes fastest.
Arguments:
- q_fresh: bfloat16 [5120, 4096], P(('groups', 'seq')), parts along dimension 0, may hold values from -9 to 9, as said below
- k_fresh: bfloat16 [5120, 4096], P(('groups', 'seq')), parts along dimension 0, may hold values from -5.6 to 5.6, as said below
- v_fresh: bfloat16 [5120, 4096], P(('groups', 'seq')), parts along dimension 0, may hold values from -6 to 6
- k_stale: bfloat16 [5120, 4096], P('groups', 'seq'), parts along dimension 0, may hold values from -5.59375 to 5.59375
- v_stale: bfloat16 [5120, 4096], P('groups', 'seq'), parts along dimension 0, may hold values from -6 to 6
- rank: int32 [10], P('groups'), parts along dimension 0, may hold values from 0 to 4, each once
- ends: int32 [10], P('groups'), parts along dimension 0, may hold values from 512 to 2560, as said below
Outputs:
- attended: bfloat16 [5120, 4096], P(('groups', 'seq')), parts along dimension 0
There are 2 independent parts, one for each index of `groups`. A program takes and returns all parts, laid end to end along the dimension named above; each array names one. Nothing has to cross between parts.
Inputs may be any that keep to these rules, and one draw needn't show every extreme that they name: `q_fresh`: queries of both draws lie within this range. `k_fresh`: keys of both draws lie within this range. Multiples of 512, never falling along the patches, ends[p] >= (p + 1) * 512; the first equals 512, the last equals 2560.
All inputs are finite; a program needn't handle non-finite values.
Results may differ from a plain program's by a relative error of at most 0.0036.
Values may be sent and summed in bfloat16 or wider, within the bound.
No kernel may reach another device: no remote copies, remote signals or barrier semaphores. Data moves between devices by JAX's collectives and lax.ppermute only.
A program may use at most 64 MiB of HBM per device.

v0:
```python
import math
import jax
import jax.numpy as jnp
from jax import lax
from jax.sharding import PartitionSpec as P

HEAD_DIM = 128
PATCH = 512


def shards(q_fresh, k_fresh, v_fresh, k_stale, v_stale, rank, ends):
    queries, keys_new, values_new = (
        lax.all_to_all(q_fresh, "seq", split_axis=1, concat_axis=0, tiled=True),
        lax.all_to_all(k_fresh, "seq", split_axis=1, concat_axis=0, tiled=True),
        lax.all_to_all(v_fresh, "seq", split_axis=1, concat_axis=0, tiled=True),
    )
    total_rows = queries.shape[0]
    width = queries.shape[1]
    heads_here = width // HEAD_DIM
    patch_count = rank.shape[0]
    scale = 1.0 / math.sqrt(HEAD_DIM)
    key_patch = jnp.arange(total_rows, dtype=jnp.int32) // PATCH
    hits = key_patch[:, None] == jnp.arange(patch_count, dtype=jnp.int32)[None, :]
    key_rank = jnp.sum(jnp.where(hits, rank[None, :], 0), axis=1)
    positions = jnp.arange(total_rows, dtype=jnp.int32)

    def split_heads(array):
        return array.reshape(array.shape[0], heads_here, HEAD_DIM)

    def one_patch(index):
        block = split_heads(lax.dynamic_slice_in_dim(queries, index * PATCH, PATCH, 0))
        my_rank = rank[index]
        limit = ends[index]
        fresh = (key_rank <= my_rank)[:, None]
        keys = split_heads(jnp.where(fresh, keys_new, k_stale))
        values = split_heads(jnp.where(fresh, values_new, v_stale))
        score = jnp.einsum("qhd,khd->hqk", block, keys, preferred_element_type=jnp.float32) * scale
        score = jnp.where((positions < limit)[None, None, :], score, -jnp.inf)
        top = jnp.max(score, axis=2, keepdims=True)
        weight = jnp.exp(score - top)
        denominator = jnp.sum(weight, axis=2)
        mixed = jnp.einsum(
            "hqk,khd->qhd", weight.astype(jnp.bfloat16), values, preferred_element_type=jnp.float32
        )
        result = mixed / jnp.transpose(denominator)[:, :, None]
        return result.reshape(PATCH, width).astype(jnp.bfloat16)

    pieces = lax.map(one_patch, jnp.arange(patch_count, dtype=jnp.int32))
    gathered = pieces.reshape(total_rows, width)
    return lax.all_to_all(gathered, "seq", split_axis=0, concat_axis=1, tiled=True)


def solution(mesh):
    return jax.shard_map(
        shards,
        mesh=mesh,
        in_specs=(
            P(("groups", "seq"), None),
            P(("groups", "seq"), None),
            P(("groups", "seq"), None),
            P("groups", "seq"),
            P("groups", "seq"),
            P("groups"),
            P("groups"),
        ),
        out_specs=P(("groups", "seq"), None),
        check_vma=False,
    )
```

profile of v0, /device:TPU:1, one launch (start us, length us, event | category | flops | bytes accessed | tf_op | source)
XLA Modules:
  0.0 222.0 jit_solution(114587770779463893)
XLA Ops:
  0.0 2.5 %copy.83 = bf16[20,16,8,256]{3,2,0,1:T(8,128)(2,1)} copy(bf16[20,16,8,256]{3,2,1,0:T(8,128)(2,1)} %bitcast.75) | data formatting | bytes 2621440 | tf_op jit(solution)/shard_map/all_to_all | solution.py:15
  2.5 7.5 %all-to-all-start = ((bf16[160,16,256]{2,0,1:T(8,128)(2,1)}), bf16[160,16,256]{2,0,1:T(8,128)(2,1)S(1)}, u32[]{:S(2)}, u32[]{:S(2)}) async-start(bf16[160,16,256]{2,0,1:T(8,128)(2,1)} %bitcast.41), calls=%async_computation | async-start | bytes 2621440 | tf_op jit(solution)/shard_map/all_to_all | solution.py:15
  11.2 26.6 %all-to-all-done = bf16[160,16,256]{2,0,1:T(8,128)(2,1)S(1)} async-done(((bf16[160,16,256]{2,0,1:T(8,128)(2,1)}), bf16[160,16,256]{2,0,1:T(8,128)(2,1)S(1)}, u32[]{:S(2)}, u32[]{:S(2)}) %all-to-all-start) | async-done | bytes 1310752 | tf_op jit(solution)/shard_map/all_to_all | solution.py:15
  37.8 7.5 %all-to-all-start.2 = ((bf16[160,16,256]{2,0,1:T(8,128)(2,1)}), bf16[160,16,256]{2,0,1:T(8,128)(2,1)S(1)}, u32[]{:S(2)}, u32[]{:S(2)}) async-start(bf16[160,16,256]{2,0,1:T(8,128)(2,1)} %bitcast.73), calls=%async_computation.2 | async-start | bytes 2621440 | tf_op jit(solution)/shard_map/all_to_all | solution.py:14
  45.3 2.5 %copy.82 = bf16[20,16,8,256]{3,2,0,1:T(8,128)(2,1)} copy(bf16[20,16,8,256]{3,2,1,0:T(8,128)(2,1)} %bitcast.77) | data formatting | bytes 2621440 | tf_op jit(solution)/shard_map/all_to_all | solution.py:13
  47.8 25.3 %all-to-all-done.2 = bf16[160,16,256]{2,0,1:T(8,128)(2,1)S(1)} async-done(((bf16[160,16,256]{2,0,1:T(8,128)(2,1)}), bf16[160,16,256]{2,0,1:T(8,128)(2,1)S(1)}, u32[]{:S(2)}, u32[]{:S(2)}) %all-to-all-start.2) | async-done | bytes 1310752 | tf_op jit(solution)/shard_map/all_to_all | solution.py:14
  74.2 7.5 %all-to-all-start.1 = ((bf16[160,16,256]{2,0,1:T(8,128)(2,1)}), bf16[160,16,256]{2,0,1:T(8,128)(2,1)}, u32[]{:S(2)}, u32[]{:S(2)}) async-start(bf16[160,16,256]{2,0,1:T(8,128)(2,1)} %bitcast.72), calls=%async_computation.1 | async-start | bytes 2621440 | tf_op jit(solution)/shard_map/all_to_all | solution.py:13
  81.7 2.4 %copy.63 = bf16[2560,256]{0,1:T(8,128)(2,1)} copy(bf16[2560,256]{1,0:T(8,128)(2,1)} %param.13) | data formatting | bytes 2621440
  84.1 1.6 copy.66
  85.9 1.6 copy.62
  87.5 1.6 copy.65
  89.1 20.6 %all-to-all-done.1 = bf16[160,16,256]{2,0,1:T(8,128)(2,1)} async-done(((bf16[160,16,256]{2,0,1:T(8,128)(2,1)}), bf16[160,16,256]{2,0,1:T(8,128)(2,1)}, u32[]{:S(2)}, u32[]{:S(2)}) %all-to-all-start.1) | async-done | bytes 1310752 | tf_op jit(solution)/shard_map/all_to_all | solution.py:13
  109.6 71.8 %while.11 = (s32[]{:T(128)}, bf16[5,512,256]{2,1,0:T(8,128)(2,1)}, s32[5]{0:T(128)S(1)}, s32[5]{0:T(128)S(1)}, s32[2560]{0:T(1024)S(1)}, /*index=5*/bf16[2560,25...) while((s32[]{:T(128)}, bf16[5,512,256]{2,1,0:T(8,128)(2,1)}, ...), condition=%wide.region_4.5_spmd.clone, body=%wide.region_1.4_spmd.clone.sunk | while | flops 1372589056 | bytes 49856844 | solution.py:48
  113.4 1.3 iota_compare_fusion.3
  116.4 1.7 fusion.43
  118.2 2.2 %fusion.44 = f32[2,512]{1,0:T(2,128)S(1)} fusion(f32[2,512,2560]{2,1,0:T(8,128)S(1)} %get-tuple-element.257, f32[2,512]{1,0:T(2,128)S(1)} %get-tuple-element.258, pred[2560]{0:T(1024)(128)(4,1)S(1)} %get-tuple-element.255), kind=kLoop, calls=%fused_computation.4.clone.1 | loop fusion | flops 10484736 | bytes 10496512 | tf_op jit(solution)/shard_map/while/body/eval_jaxpr/reduce_sum | solution.py:41
  120.4 2.7 %fusion.45 = bf16[512,2,128]{0,2,1:T(8,128)(2,1)S(1)} fusion(f32[2,512,2560]{2,1,0:T(8,128)S(1)} %get-tuple-element.257, f32[2,512]{1,0:T(2,128)S(1)} %get-tuple-element.258, pred[2560]{0:T(1024)(128)(4,1)S(1)} %get-tuple-element.255, bf16[2560,2,128]{0,2,1:T(8,128)(2,1)S(1)} %bitcast.79, bf16[2560,2,128]{0,2,1:T(8,128)(2,1)S(1)} %bitcast.78, ...), kind=kOutput, calls=%fused_computation.15.clone.1 | convolution fusion | flops 682491904 | bytes 13382656 | tf_op jit(solution)/shard_map/while/body/eval_jaxpr/hqk,khd->qhd/dot_general | solution.py:42
  127.8 1.3 iota_compare_fusion.3
  130.8 1.7 fusion.43
  132.5 2.2 %fusion.44 = f32[2,512]{1,0:T(2,128)S(1)} fusion(f32[2,512,2560]{2,1,0:T(8,128)S(1)} %get-tuple-element.257, f32[2,512]{1,0:T(2,128)S(1)} %get-tuple-element.258, pred[2560]{0:T(1024)(128)(4,1)S(1)} %get-tuple-element.255), kind=kLoop, calls=%fused_computation.4.clone.1 | loop fusion | flops 10484736 | bytes 10496512 | tf_op jit(solution)/shard_map/while/body/eval_jaxpr/reduce_sum | solution.py:41
  134.8 2.7 %fusion.45 = bf16[512,2,128]{0,2,1:T(8,128)(2,1)S(1)} fusion(f32[2,512,2560]{2,1,0:T(8,128)S(1)} %get-tuple-element.257, f32[2,512]{1,0:T(2,128)S(1)} %get-tuple-element.258, pred[2560]{0:T(1024)(128)(4,1)S(1)} %get-tuple-element.255, bf16[2560,2,128]{0,2,1:T(8,128)(2,1)S(1)} %bitcast.79, bf16[2560,2,128]{0,2,1:T(8,128)(2,1)S(1)} %bitcast.78, ...), kind=kOutput, calls=%fused_computation.15.clone.1 | convolution fusion | flops 682491904 | bytes 13382656 | tf_op jit(solution)/shard_map/while/body/eval_jaxpr/hqk,khd->qhd/dot_general | solution.py:42
  142.1 1.3 iota_compare_fusion.3
  145.2 1.7 fusion.43
  146.9 2.2 %fusion.44 = f32[2,512]{1,0:T(2,128)S(1)} fusion(f32[2,512,2560]{2,1,0:T(8,128)S(1)} %get-tuple-element.257, f32[2,512]{1,0:T(2,128)S(1)} %get-tuple-element.258, pred[2560]{0:T(1024)(128)(4,1)S(1)} %get-tuple-element.255), kind=kLoop, calls=%fused_computation.4.clone.1 | loop fusion | flops 10484736 | bytes 10496512 | tf_op jit(solution)/shard_map/while/body/eval_jaxpr/reduce_sum | solution.py:41
  149.2 2.7 %fusion.45 = bf16[512,2,128]{0,2,1:T(8,128)(2,1)S(1)} fusion(f32[2,512,2560]{2,1,0:T(8,128)S(1)} %get-tuple-element.257, f32[2,512]{1,0:T(2,128)S(1)} %get-tuple-element.258, pred[2560]{0:T(1024)(128)(4,1)S(1)} %get-tuple-element.255, bf16[2560,2,128]{0,2,1:T(8,128)(2,1)S(1)} %bitcast.79, bf16[2560,2,128]{0,2,1:T(8,128)(2,1)S(1)} %bitcast.78, ...), kind=kOutput, calls=%fused_computation.15.clone.1 | convolution fusion | flops 682491904 | bytes 13382656 | tf_op jit(solution)/shard_map/while/body/eval_jaxpr/hqk,khd->qhd/dot_general | solution.py:42
  159.5 1.7 fusion.43
  161.3 2.2 %fusion.44 = f32[2,512]{1,0:T(2,128)S(1)} fusion(f32[2,512,2560]{2,1,0:T(8,128)S(1)} %get-tuple-element.257, f32[2,512]{1,0:T(2,128)S(1)} %get-tuple-element.258, pred[2560]{0:T(1024)(128)(4,1)S(1)} %get-tuple-element.255), kind=kLoop, calls=%fused_computation.4.clone.1 | loop fusion | flops 10484736 | bytes 10496512 | tf_op jit(solution)/shard_map/while/body/eval_jaxpr/reduce_sum | solution.py:41
  163.5 2.7 %fusion.45 = bf16[512,2,128]{0,2,1:T(8,128)(2,1)S(1)} fusion(f32[2,512,2560]{2,1,0:T(8,128)S(1)} %get-tuple-element.257, f32[2,512]{1,0:T(2,128)S(1)} %get-tuple-element.258, pred[2560]{0:T(1024)(128)(4,1)S(1)} %get-tuple-element.255, bf16[2560,2,128]{0,2,1:T(8,128)(2,1)S(1)} %bitcast.79, bf16[2560,2,128]{0,2,1:T(8,128)(2,1)S(1)} %bitcast.78, ...), kind=kOutput, calls=%fused_computation.15.clone.1 | convolution fusion | flops 682491904 | bytes 13382656 | tf_op jit(solution)/shard_map/while/body/eval_jaxpr/hqk,khd->qhd/dot_general | solution.py:42
  173.9 1.7 fusion.43
  175.6 2.2 %fusion.44 = f32[2,512]{1,0:T(2,128)S(1)} fusion(f32[2,512,2560]{2,1,0:T(8,128)S(1)} %get-tuple-element.257, f32[2,512]{1,0:T(2,128)S(1)} %get-tuple-element.258, pred[2560]{0:T(1024)(128)(4,1)S(1)} %get-tuple-element.255), kind=kLoop, calls=%fused_computation.4.clone.1 | loop fusion | flops 10484736 | bytes 10496512 | tf_op jit(solution)/shard_map/while/body/eval_jaxpr/reduce_sum | solution.py:41
  177.9 2.7 %fusion.45 = bf16[512,2,128]{0,2,1:T(8,128)(2,1)S(1)} fusion(f32[2,512,2560]{2,1,0:T(8,128)S(1)} %get-tuple-element.257, f32[2,512]{1,0:T(2,128)S(1)} %get-tuple-element.258, pred[2560]{0:T(1024)(128)(4,1)S(1)} %get-tuple-element.255, bf16[2560,2,128]{0,2,1:T(8,128)(2,1)S(1)} %bitcast.79, bf16[2560,2,128]{0,2,1:T(8,128)(2,1)S(1)} %bitcast.78, ...), kind=kOutput, calls=%fused_computation.15.clone.1 | convolution fusion | flops 682491904 | bytes 13382656 | tf_op jit(solution)/shard_map/while/body/eval_jaxpr/hqk,khd->qhd/dot_general | solution.py:42
  181.5 39.3 %all_to_all.76 = bf16[16,160,256]{2,1,0:T(8,128)(2,1)S(1)} all-to-all(bf16[16,160,256]{2,1,0:T(8,128)(2,1)} %bitcast.80), channel_id=1, replica_groups=mesh['groups'=2,'seq'=16] {'seq'}, dimensions={0} | all-to-all | bytes 2621440 | tf_op jit(solution)/shard_map/all_to_all | solution.py:50
  (71 shorter events, 25.6 us)
Async XLA Ops:
  2.5 7.5 %copy-start.1 = (bf16[160,4096]{1,0:T(8,128)(2,1)S(1)}, bf16[160,4096]{1,0:T(8,128)(2,1)}, u32[]{:S(2)}) copy-start(bf16[160,4096]{1,0:T(8,128)(2,1)} %param.10) | copy-start | bytes 3932164
  2.5 35.3 %all-to-all-start = ((bf16[160,16,256]{2,0,1:T(8,128)(2,1)}), bf16[160,16,256]{2,0,1:T(8,128)(2,1)S(1)}, u32[]{:S(2)}, u32[]{:S(2)}) async-start(bf16[160,16,256]{2,0,1:T(8,128)(2,1)} %bitcast.41), calls=%async_computation | async-start | bytes 2621440 | tf_op jit(solution)/shard_map/all_to_all | solution.py:15
  37.8 35.3 %all-to-all-start.2 = ((bf16[160,16,256]{2,0,1:T(8,128)(2,1)}), bf16[160,16,256]{2,0,1:T(8,128)(2,1)S(1)}, u32[]{:S(2)}, u32[]{:S(2)}) async-start(bf16[160,16,256]{2,0,1:T(8,128)(2,1)} %bitcast.73), calls=%async_computation.2 | async-start | bytes 2621440 | tf_op jit(solution)/shard_map/all_to_all | solution.py:14
  73.1 1.1 copy-start
  74.2 35.4 %all-to-all-start.1 = ((bf16[160,16,256]{2,0,1:T(8,128)(2,1)}), bf16[160,16,256]{2,0,1:T(8,128)(2,1)}, u32[]{:S(2)}, u32[]{:S(2)}) async-start(bf16[160,16,256]{2,0,1:T(8,128)(2,1)} %bitcast.72), calls=%async_computation.1 | async-start | bytes 2621440 | tf_op jit(solution)/shard_map/all_to_all | solution.py:13
  84.1 1.6 copy-start.4
  87.5 22.2 %copy-start.5 = (s32[5]{0:T(128)S(1)}, s32[5]{0:T(128)}, u32[]{:S(2)}) copy-start(s32[5]{0:T(128)} %param.15) | copy-start | bytes 64
  118.1 2.3 %copy-start.2 = (bf16[2560,256]{0,1:T(8,128)(2,1)S(1)}, bf16[2560,256]{0,1:T(8,128)(2,1)}, u32[]{:S(2)}) copy-start(bf16[2560,256]{0,1:T(8,128)(2,1)} %get-tuple-element.297) | copy-start | bytes 3932164 | tf_op jit(solution)/shard_map/while
  118.2 2.3 %copy-start.3 = (bf16[2560,256]{0,1:T(8,128)(2,1)S(1)}, bf16[2560,256]{0,1:T(8,128)(2,1)}, u32[]{:S(2)}) copy-start(bf16[2560,256]{0,1:T(8,128)(2,1)} %get-tuple-element.296) | copy-start | bytes 3932164 | tf_op jit(solution)/shard_map/while
  132.5 2.3 %copy-start.2 = (bf16[2560,256]{0,1:T(8,128)(2,1)S(1)}, bf16[2560,256]{0,1:T(8,128)(2,1)}, u32[]{:S(2)}) copy-start(bf16[2560,256]{0,1:T(8,128)(2,1)} %get-tuple-element.297) | copy-start | bytes 3932164 | tf_op jit(solution)/shard_map/while
  132.5 2.3 %copy-start.3 = (bf16[2560,256]{0,1:T(8,128)(2,1)S(1)}, bf16[2560,256]{0,1:T(8,128)(2,1)}, u32[]{:S(2)}) copy-start(bf16[2560,256]{0,1:T(8,128)(2,1)} %get-tuple-element.296) | copy-start | bytes 3932164 | tf_op jit(solution)/shard_map/while
  146.9 2.3 %copy-start.2 = (bf16[2560,256]{0,1:T(8,128)(2,1)S(1)}, bf16[2560,256]{0,1:T(8,128)(2,1)}, u32[]{:S(2)}) copy-start(bf16[2560,256]{0,1:T(8,128)(2,1)} %get-tuple-element.297) | copy-start | bytes 3932164 | tf_op jit(solution)/shard_map/while
  146.9 2.3 %copy-start.3 = (bf16[2560,256]{0,1:T(8,128)(2,1)S(1)}, bf16[2560,256]{0,1:T(8,128)(2,1)}, u32[]{:S(2)}) copy-start(bf16[2560,256]{0,1:T(8,128)(2,1)} %get-tuple-element.296) | copy-start | bytes 3932164 | tf_op jit(solution)/shard_map/while
  161.3 2.3 %copy-start.2 = (bf16[2560,256]{0,1:T(8,128)(2,1)S(1)}, bf16[2560,256]{0,1:T(8,128)(2,1)}, u32[]{:S(2)}) copy-start(bf16[2560,256]{0,1:T(8,128)(2,1)} %get-tuple-element.297) | copy-start | bytes 3932164 | tf_op jit(solution)/shard_map/while
  161.3 2.3 %copy-start.3 = (bf16[2560,256]{0,1:T(8,128)(2,1)S(1)}, bf16[2560,256]{0,1:T(8,128)(2,1)}, u32[]{:S(2)}) copy-start(bf16[2560,256]{0,1:T(8,128)(2,1)} %get-tuple-element.296) | copy-start | bytes 3932164 | tf_op jit(solution)/shard_map/while
  175.6 2.3 %copy-start.2 = (bf16[2560,256]{0,1:T(8,128)(2,1)S(1)}, bf16[2560,256]{0,1:T(8,128)(2,1)}, u32[]{:S(2)}) copy-start(bf16[2560,256]{0,1:T(8,128)(2,1)} %get-tuple-element.297) | copy-start | bytes 3932164 | tf_op jit(solution)/shard_map/while
  175.6 2.3 %copy-start.3 = (bf16[2560,256]{0,1:T(8,128)(2,1)S(1)}, bf16[2560,256]{0,1:T(8,128)(2,1)}, u32[]{:S(2)}) copy-start(bf16[2560,256]{0,1:T(8,128)(2,1)} %get-tuple-element.296) | copy-start | bytes 3932164 | tf_op jit(solution)/shard_map/while
where the time goes:
time: 223 us; the launch traced here: 222 us
  waiting for transfers between devices  72.5 us (33%)
  blocking collectives  39.3 us (18%)
  local copies, waits for them, and re-layouts  35.2 us (16%)
  starting transfers between devices  22.4 us (10%)
  matrix products  22.2 us (10%)
  other arithmetic  17.6 us (8%)
  loops' own time  12.7 us (6%)
    all_to_all x1, blocking collectives, shards(): lax.all_to_all(gathered, 'seq', split_axis=0, concat_axis=1, tiled=True)  39.3 us
    all_to_all x1, waiting for transfers between devices, shards(): lax.all_to_all(v_fresh, 'seq', split_axis=1, concat_axis=0, tiled=True)  26.6 us
    all_to_all x1, waiting for transfers between devices, shards(): lax.all_to_all(k_fresh, 'seq', split_axis=1, concat_axis=0, tiled=True)  25.3 us
    all_to_all x1, waiting for transfers between devices, shards(): lax.all_to_all(q_fresh, 'seq', split_axis=1, concat_axis=0, tiled=True)  20.6 us
    dot_general x5, matrix products, one_patch(): jnp.einsum('hqk,khd->qhd', weight.astype(jnp.bfloat16), values, preferred...  13.6 us
    another operation x1, loops' own time, shards(): pieces = lax.map(one_patch, jnp.arange(patch_count, dtype=jnp.int32))  12.7 us
    reduce_sum x5, other arithmetic, one_patch(): denominator = jnp.sum(weight, axis=2)  11.2 us
    dot_general x5, matrix products, one_patch(): jnp.einsum('qhd,khd->hqk', block, keys, preferred_element_type=jnp.float32)  8.59 us
  transfers between devices with their start and end apart: 3, of which 3 were waited for; matrix products, arithmetic and copies ran while one was open for 5% of the time, Pallas kernels for 0%

commit v1 on v0

--- a/solution.py
+++ b/solution.py
@@ -8,11 +8,19 @@
 PATCH = 512
 
 
+def trace_racks(incoming_x):
+    answer = lax.psum(1, "seq")
+    mixed_arr = jnp.split(incoming_x, answer, axis=1)
+    work_now = jnp.stack(mixed_arr)
+    known = lax.all_to_all(work_now, "seq", 0, 0)
+    return jnp.concatenate(known, axis=0)
+
+
 def shards(q_fresh, k_fresh, v_fresh, k_stale, v_stale, rank, ends):
     queries, keys_new, values_new = (
         lax.all_to_all(q_fresh, "seq", split_axis=1, concat_axis=0, tiled=True),
         lax.all_to_all(k_fresh, "seq", split_axis=1, concat_axis=0, tiled=True),
-        lax.all_to_all(v_fresh, "seq", split_axis=1, concat_axis=0, tiled=True),
+        trace_racks(v_fresh),
     )
     total_rows = queries.shape[0]
     width = queries.shape[1]

time: 223 us -> 245 us (1.099)
  local copies, waits for them, and re-layouts: 35.2 us -> 57.1 us
    unnamed x12 -> x27, local copies, waits for them, and re-layouts: 8.36 us -> 31.3 us
    all_to_all x1 -> x0, local copies, waits for them, and re-layouts: 2.51 us -> none  [shards(): lax.all_to_all(v_fresh, 'seq', split_axis=1, concat_axis=0, tiled=True)]
where the time goes in v1:
time: 245 us; the launch traced here: 244 us
  waiting for transfers between devices  72.5 us (30%)
  local copies, waits for them, and re-layouts  57.1 us (23%)
  blocking collectives  39.3 us (16%)
  starting transfers between devices  22.4 us (9%)
  matrix products  22.2 us (9%)
  other arithmetic  17.6 us (7%)
  loops' own time  12.8 us (5%)
    all_to_all x1, blocking collectives, shards(): lax.all_to_all(gathered, 'seq', split_axis=0, concat_axis=1, tiled=True)  39.3 us
    unnamed x27, local copies, waits for them, and re-layouts  31.3 us
    all_to_all x1, waiting for transfers between devices, trace_racks(): known = lax.all_to_all(work_now, 'seq', 0, 0)  26.6 us
    all_to_all x1, waiting for transfers between devices, shards(): lax.all_to_all(k_fresh, 'seq', split_axis=1, concat_axis=0, tiled=True)  25.3 us
    all_to_all x1, waiting for transfers between devices, shards(): lax.all_to_all(q_fresh, 'seq', split_axis=1, concat_axis=0, tiled=True)  20.6 us
    dot_general x5, matrix products, one_patch(): jnp.einsum('hqk,khd->qhd', weight.astype(jnp.bfloat16), values, preferred...  13.6 us
    another operation x1, loops' own time, shards(): pieces = lax.map(one_patch, jnp.arange(patch_count, dtype=jnp.int32))  12.8 us
    reduce_sum x5, other arithmetic, one_patch(): denominator = jnp.sum(weight, axis=2)  11.2 us
  transfers between devices with their start and end apart: 3, of which 3 were waited for; matrix products, arithmetic and copies ran while one was open for 5% of the time, Pallas kernels for 0%

profile of v1, /device:TPU:1, one launch (start us, length us, event | category | flops | bytes accessed | tf_op | source)
XLA Modules:
  0.0 243.9 jit_solution(10480382787907858958)
XLA Ops:
  0.0 1.5 bitcast_dynamic-update-slice_fusion.15
  1.5 1.5 bitcast_dynamic-update-slice_fusion.14
  3.1 1.5 bitcast_dynamic-update-slice_fusion.13
  4.6 1.5 bitcast_dynamic-update-slice_fusion.12
  24.4 7.5 %all-to-all-start = ((bf16[16,160,256]{2,1,0:T(8,128)(2,1)}), bf16[16,160,256]{2,1,0:T(8,128)(2,1)S(1)}, u32[]{:S(2)}, u32[]{:S(2)}) async-start(bf16[16,160,256]{2,1,0:T(8,128)(2,1)} %bitcast_dynamic-update-slice_fusion), calls=%async_computation | async-start | bytes 2621440 | tf_op jit(solution)/shard_map/all_to_all | solution.py:15
  33.1 26.6 %all-to-all-done = bf16[16,160,256]{2,1,0:T(8,128)(2,1)S(1)} async-done(((bf16[16,160,256]{2,1,0:T(8,128)(2,1)}), bf16[16,160,256]{2,1,0:T(8,128)(2,1)S(1)}, u32[]{:S(2)}, u32[]{:S(2)}) %all-to-all-start) | async-done | bytes 1310752 | tf_op jit(solution)/shard_map/all_to_all | solution.py:15
  59.7 7.5 %all-to-all-start.2 = ((bf16[160,16,256]{2,0,1:T(8,128)(2,1)}), bf16[160,16,256]{2,0,1:T(8,128)(2,1)S(1)}, u32[]{:S(2)}, u32[]{:S(2)}) async-start(bf16[160,16,256]{2,0,1:T(8,128)(2,1)} %bitcast.99), calls=%async_computation.2 | async-start | bytes 2621440 | tf_op jit(solution)/shard_map/all_to_all | solution.py:22
  67.2 2.5 %copy.76 = bf16[20,16,8,256]{3,2,0,1:T(8,128)(2,1)} copy(bf16[20,16,8,256]{3,2,1,0:T(8,128)(2,1)} %bitcast.102) | data formatting | bytes 2621440 | tf_op jit(solution)/shard_map/all_to_all | solution.py:21
  69.7 25.3 %all-to-all-done.2 = bf16[160,16,256]{2,0,1:T(8,128)(2,1)S(1)} async-done(((bf16[160,16,256]{2,0,1:T(8,128)(2,1)}), bf16[160,16,256]{2,0,1:T(8,128)(2,1)S(1)}, u32[]{:S(2)}, u32[]{:S(2)}) %all-to-all-start.2) | async-done | bytes 1310752 | tf_op jit(solution)/shard_map/all_to_all | solution.py:22
  96.2 7.5 %all-to-all-start.1 = ((bf16[160,16,256]{2,0,1:T(8,128)(2,1)}), bf16[160,16,256]{2,0,1:T(8,128)(2,1)}, u32[]{:S(2)}, u32[]{:S(2)}) async-start(bf16[160,16,256]{2,0,1:T(8,128)(2,1)} %bitcast.98), calls=%async_computation.1 | async-start | bytes 2621440 | tf_op jit(solution)/shard_map/all_to_all | solution.py:21
  103.6 2.4 copy.59
  106.1 1.6 copy.62
  107.8 1.6 copy.58
  109.4 1.6 copy.61
  111.0 20.6 %all-to-all-done.1 = bf16[160,16,256]{2,0,1:T(8,128)(2,1)} async-done(((bf16[160,16,256]{2,0,1:T(8,128)(2,1)}), bf16[160,16,256]{2,0,1:T(8,128)(2,1)}, u32[]{:S(2)}, u32[]{:S(2)}) %all-to-all-start.1) | async-done | bytes 1310752 | tf_op jit(solution)/shard_map/all_to_all | solution.py:21
  131.6 71.8 %while.11 = (s32[]{:T(128)}, bf16[5,512,256]{2,1,0:T(8,128)(2,1)}, s32[5]{0:T(128)S(1)}, s32[5]{0:T(128)S(1)}, s32[2560]{0:T(1024)S(1)}, /*index=5*/bf16[2560,25...) while((s32[]{:T(128)}, bf16[5,512,256]{2,1,0:T(8,128)(2,1)}, ...), condition=%wide.region_4.5_spmd.clone, body=%wide.region_1.4_spmd.clone.sunk | while | flops 1372589056 | bytes 49856844 | solution.py:56
  138.4 1.7 fusion.43
  140.1 2.2 fusion.44
  142.3 2.7 %fusion.45 = bf16[512,2,128]{0,2,1:T(8,128)(2,1)S(1)} fusion(f32[2,512,2560]{2,1,0:T(8,128)S(1)} %get-tuple-element.257, f32[2,512]{1,0:T(2,128)S(1)} %get-tuple-element.258, pred[2560]{0:T(1024)(128)(4,1)S(1)} %get-tuple-element.255, bf16[2560,2,128]{0,2,1:T(8,128)(2,1)S(1)} %bitcast.104, bf16[2560,2,128]{0,2,1:T(8,128)(2,1)S(1)} %bitcast.103, ...), kind=kOutput, calls=%fused_computation.15.clone.1 | convolution fusion | flops 682491904 | bytes 13382656 | tf_op jit(solution)/shard_map/while/body/eval_jaxpr/hqk,khd->qhd/dot_general | solution.py:50
  152.7 1.7 fusion.43
  154.5 2.2 fusion.44
  156.7 2.7 %fusion.45 = bf16[512,2,128]{0,2,1:T(8,128)(2,1)S(1)} fusion(f32[2,512,2560]{2,1,0:T(8,128)S(1)} %get-tuple-element.257, f32[2,512]{1,0:T(2,128)S(1)} %get-tuple-element.258, pred[2560]{0:T(1024)(128)(4,1)S(1)} %get-tuple-element.255, bf16[2560,2,128]{0,2,1:T(8,128)(2,1)S(1)} %bitcast.104, bf16[2560,2,128]{0,2,1:T(8,128)(2,1)S(1)} %bitcast.103, ...), kind=kOutput, calls=%fused_computation.15.clone.1 | convolution fusion | flops 682491904 | bytes 13382656 | tf_op jit(solution)/shard_map/while/body/eval_jaxpr/hqk,khd->qhd/dot_general | solution.py:50
  167.1 1.7 fusion.43
  168.8 2.2 fusion.44
  171.1 2.7 %fusion.45 = bf16[512,2,128]{0,2,1:T(8,128)(2,1)S(1)} fusion(f32[2,512,2560]{2,1,0:T(8,128)S(1)} %get-tuple-element.257, f32[2,512]{1,0:T(2,128)S(1)} %get-tuple-element.258, pred[2560]{0:T(1024)(128)(4,1)S(1)} %get-tuple-element.255, bf16[2560,2,128]{0,2,1:T(8,128)(2,1)S(1)} %bitcast.104, bf16[2560,2,128]{0,2,1:T(8,128)(2,1)S(1)} %bitcast.103, ...), kind=kOutput, calls=%fused_computation.15.clone.1 | convolution fusion | flops 682491904 | bytes 13382656 | tf_op jit(solution)/shard_map/while/body/eval_jaxpr/hqk,khd->qhd/dot_general | solution.py:50
  181.5 1.7 fusion.43
  183.2 2.2 fusion.44
  185.4 2.7 %fusion.45 = bf16[512,2,128]{0,2,1:T(8,128)(2,1)S(1)} fusion(f32[2,512,2560]{2,1,0:T(8,128)S(1)} %get-tuple-element.257, f32[2,512]{1,0:T(2,128)S(1)} %get-tuple-element.258, pred[2560]{0:T(1024)(128)(4,1)S(1)} %get-tuple-element.255, bf16[2560,2,128]{0,2,1:T(8,128)(2,1)S(1)} %bitcast.104, bf16[2560,2,128]{0,2,1:T(8,128)(2,1)S(1)} %bitcast.103, ...), kind=kOutput, calls=%fused_computation.15.clone.1 | convolution fusion | flops 682491904 | bytes 13382656 | tf_op jit(solution)/shard_map/while/body/eval_jaxpr/hqk,khd->qhd/dot_general | solution.py:50
  195.8 1.7 fusion.43
  197.6 2.2 fusion.44
  199.8 2.7 %fusion.45 = bf16[512,2,128]{0,2,1:T(8,128)(2,1)S(1)} fusion(f32[2,512,2560]{2,1,0:T(8,128)S(1)} %get-tuple-element.257, f32[2,512]{1,0:T(2,128)S(1)} %get-tuple-element.258, pred[2560]{0:T(1024)(128)(4,1)S(1)} %get-tuple-element.255, bf16[2560,2,128]{0,2,1:T(8,128)(2,1)S(1)} %bitcast.104, bf16[2560,2,128]{0,2,1:T(8,128)(2,1)S(1)} %bitcast.103, ...), kind=kOutput, calls=%fused_computation.15.clone.1 | convolution fusion | flops 682491904 | bytes 13382656 | tf_op jit(solution)/shard_map/while/body/eval_jaxpr/hqk,khd->qhd/dot_general | solution.py:50
  203.4 39.3 %all_to_all.62 = bf16[16,160,256]{2,1,0:T(8,128)(2,1)S(1)} all-to-all(bf16[16,160,256]{2,1,0:T(8,128)(2,1)} %bitcast.105), channel_id=1, replica_groups=mesh['groups'=2,'seq'=16] {'seq'}, dimensions={0} | all-to-all | bytes 2621440 | tf_op jit(solution)/shard_map/all_to_all | solution.py:58
  (86 shorter events, 47.7 us)
Async XLA Ops:
  24.4 7.5 %copy-start.1 = (bf16[160,4096]{1,0:T(8,128)(2,1)S(1)}, bf16[160,4096]{1,0:T(8,128)(2,1)}, u32[]{:S(2)}) copy-start(bf16[160,4096]{1,0:T(8,128)(2,1)} %param.10) | copy-start | bytes 3932164
  24.4 35.3 %all-to-all-start = ((bf16[16,160,256]{2,1,0:T(8,128)(2,1)}), bf16[16,160,256]{2,1,0:T(8,128)(2,1)S(1)}, u32[]{:S(2)}, u32[]{:S(2)}) async-start(bf16[16,160,256]{2,1,0:T(8,128)(2,1)} %bitcast_dynamic-update-slice_fusion), calls=%async_computation | async-start | bytes 2621440 | tf_op jit(solution)/shard_map/all_to_all | solution.py:15
  59.7 35.3 %all-to-all-start.2 = ((bf16[160,16,256]{2,0,1:T(8,128)(2,1)}), bf16[160,16,256]{2,0,1:T(8,128)(2,1)S(1)}, u32[]{:S(2)}, u32[]{:S(2)}) async-start(bf16[160,16,256]{2,0,1:T(8,128)(2,1)} %bitcast.99), calls=%async_computation.2 | async-start | bytes 2621440 | tf_op jit(solution)/shard_map/all_to_all | solution.py:22
  95.0 1.1 copy-start
  96.2 35.4 %all-to-all-start.1 = ((bf16[160,16,256]{2,0,1:T(8,128)(2,1)}), bf16[160,16,256]{2,0,1:T(8,128)(2,1)}, u32[]{:S(2)}, u32[]{:S(2)}) async-start(bf16[160,16,256]{2,0,1:T(8,128)(2,1)} %bitcast.98), calls=%async_computation.1 | async-start | bytes 2621440 | tf_op jit(solution)/shard_map/all_to_all | solution.py:21
  106.1 1.6 copy-start.4
  109.4 22.2 %copy-start.5 = (s32[5]{0:T(128)S(1)}, s32[5]{0:T(128)}, u32[]{:S(2)}) copy-start(s32[5]{0:T(128)} %param.15) | copy-start | bytes 64
  140.1 2.3 copy-start.2
  140.1 2.3 copy-start.3
  154.4 2.3 copy-start.2
  154.4 2.3 copy-start.3
  168.8 2.3 copy-start.2
  168.8 2.3 copy-start.3
  183.2 2.3 copy-start.2
  183.2 2.3 copy-start.3
  197.5 2.3 copy-start.2
  197.5 2.3 copy-start.3
